TPU v7x, 256 devices: a whole 4x4x8 slice. The times are simulated.
256 devices in a mesh: pipe: 2 (over core), slab: 8 (over x, z_hi), dp: 16 (over z_lo, y).
Axes of the slice: x: 4, y: 4, z: 8 (z_hi: 2, z_lo: 4; z = z_hi * 4 + z_lo), core: 2. Of those that a mesh axis runs over, the one named last changes fastest.
Arguments:
- saved_inputs: bfloat16 [2, 2, 16, 2, 16, 16, 512], P('pipe', None, 'dp', None, 'slab'), may hold values from -12 to 12
- loss_cotangent: bfloat16 [2, 16, 2, 16, 16, 512], P(None, 'dp', None, 'slab'), may hold values from -3 to 3
- upstream: bfloat16 [16, 2, 16, 16, 512], P('dp', None, 'slab'), may hold values from -3 to 3
- conv_weight: bfloat16 [2, 512, 13824], P('pipe', 'dp'), may hold values from -0.0546875 to 0.0546875
- adagn_table: bfloat16 [2, 1000, 1024], P('pipe'), may hold values from -3 to 3
- timesteps: int32 [3, 16], P(None, 'dp'), may hold values from 0 to 999
- frame_counts: int32 [3, 16], P(None, 'dp'), may hold values from 1 to 2
Outputs:
- input_grads: bfloat16 [2, 2, 16, 2, 16, 16, 512], P('pipe', None, 'dp', None, 'slab')
- weight_grad: float32 [2, 512, 13824], P('pipe', 'dp')
- embed_grad: float32 [2, 2, 16, 1024], P('pipe', None, 'dp')
All inputs are finite; a program needn't handle non-finite values.
Results may differ from a plain program's by a relative error of at most 0.015.
Values may be sent and summed in bfloat16 or wider, within the bound.
A program may use at most 128 MiB of HBM per device.

v0:
```python
import math
import jax
import jax.numpy as jnp
from jax import lax
from jax.sharding import PartitionSpec as P

GROUPS = 32
EPS = 1e-05


def extended(x, sides, width):
    for axis, dim in sides:
        devices, length = (lax.axis_size(axis), x.shape[dim])
        up = [(i, (i + 1) % devices) for i in range(devices - 1)]
        down = [(j, i) for i, j in up]
        last = lax.slice_in_dim(x, length - width, length, axis=dim)
        initial = lax.slice_in_dim(x, 0, width, axis=dim)
        before = lax.ppermute(last, axis, up)
        after = lax.ppermute(initial, axis, down)
        x = jnp.concatenate([before, x, after], axis=dim)
    return x


def shifted(block, axis, distance):
    devices = range(lax.axis_size(axis))
    route = [(i - distance, i) for i in devices if i - distance in devices]
    return lax.ppermute(block, axis, route)


def group_sums(values, groups):
    summed = jnp.sum(values.reshape(-1, values.shape[-1]), axis=0)
    return jnp.sum(summed.reshape(groups, -1), axis=1)


def silu_grad(preact):
    sigma = jax.nn.sigmoid(preact)
    return sigma * (1.0 + preact * (1.0 - sigma))


def hidden_of(values, mean_c, rstd_c, gain_row, bias_row, mask_now):
    normed = (values - mean_c) * rstd_c
    preact = normed * gain_row + bias_row
    activated = jax.nn.silu(preact) * mask_now[:, None, None, None]
    return (normed, preact, activated)


def norm_terms(moment_one, moment_two, count_now):
    mean_g = moment_one / count_now
    var_g = moment_two / count_now - mean_g * mean_g
    return (mean_g, lax.rsqrt(var_g + EPS))


def tap_stack(padded, frames, slab_rows, cells_wide, mirrored):
    slices = []
    for depth_at in range(3):
        for vertical in range(3):
            for across in range(3):
                if mirrored:
                    offsets = (2 - depth_at, 2 - vertical, 2 - across)
                else:
                    offsets = (depth_at, vertical, across)
                slices.append(
                    padded[
                        ...,
                        offsets[0] : offsets[0] + frames,
                        offsets[1] : offsets[1] + slab_rows,
                        offsets[2] : offsets[2] + cells_wide,
                        :,
                    ]
                )
    return jnp.stack(slices, 0)


def pad_cells(values):
    return jnp.pad(values, ((1, 1), (0, 0), (1, 1), (0, 0)))


def local(
    saved_inputs, loss_cotangent, upstream, conv_weight, adagn_table, timesteps, frame_counts
):
    section_index = lax.axis_index("pipe")
    slab_count = lax.axis_size("slab")
    replicas = lax.axis_size("dp")
    inputs = saved_inputs[0, :, 0]
    tick_count, frames, slab_rows, cells_wide, channels = inputs.shape
    groups = GROUPS
    per_group = channels // groups
    height_total = slab_rows * slab_count
    step_table = adagn_table[0]
    weight_local = conv_weight[0]
    steps_now = lax.dynamic_slice_in_dim(timesteps[:, 0], section_index, tick_count)
    counts_now = lax.dynamic_slice_in_dim(frame_counts[:, 0], section_index, tick_count)
    onehot = (
        steps_now[:, None] == jnp.arange(step_table.shape[0], dtype=jnp.int32)[None, :]
    ).astype(jnp.bfloat16)
    embedded = jnp.dot(onehot, step_table, preferred_element_type=jnp.float32)
    scales = 1.0 + embedded[:, :channels]
    shifts = embedded[:, channels:]
    frame_masks = (jnp.arange(frames, dtype=jnp.int32)[None, :] < counts_now[:, None]).astype(
        jnp.float32
    )
    valid_counts = counts_now.astype(jnp.float32) * float(height_total * cells_wide * per_group)
    weight_norm = 1.0 / math.sqrt(tick_count * replicas * frames * height_total * cells_wide)
    embed_norm = 1.0 / math.sqrt(frames * height_total * cells_wide)
    full_weight = lax.all_gather(weight_local, "dp", axis=0, tiled=True).reshape(
        channels, 27, channels
    )
    dx_list = []
    embed_list = []
    hidden_exts = []
    cotangents = []
    received = None
    for tick_index in range(tick_count):
        values = inputs[tick_index].astype(jnp.float32)
        masked = values * frame_masks[tick_index][:, None, None, None]
        part_one = group_sums(masked, groups)
        part_two = group_sums(masked * values, groups)
        moment_one, moment_two = lax.psum((part_one, part_two), "slab")
        count_now = valid_counts[tick_index]
        mean_g, rstd_g = norm_terms(moment_one, moment_two, count_now)
        mean_c = jnp.repeat(mean_g, per_group)
        rstd_c = jnp.repeat(rstd_g, per_group)
        mask_now = frame_masks[tick_index]
        normed, preact, activated = hidden_of(
            inputs[tick_index].astype(jnp.float32),
            mean_c,
            rstd_c,
            scales[tick_index],
            shifts[tick_index],
            mask_now,
        )
        hidden_ext = extended(activated.astype(jnp.bfloat16), (("slab", 1),), 1)
        hidden_exts.append(hidden_ext)
        incoming = upstream[0] if tick_index == 0 else received
        cotangent = jnp.where(section_index == 1, loss_cotangent[tick_index, 0], incoming)
        cot_rows = extended(cotangent, (("slab", 1),), 1)
        cot_pad = pad_cells(cot_rows)
        tap_slices = tap_stack(cot_pad, frames, slab_rows, cells_wide, True)
        upward = jnp.einsum(
            "tfrwo,oti->frwi", tap_slices, full_weight, preferred_element_type=jnp.float32
        )
        pre_grad = upward * silu_grad(preact) * mask_now[:, None, None, None]
        dnormed = pre_grad * scales[tick_index]
        part_a = group_sums(dnormed, groups)
        part_b = group_sums(dnormed * normed, groups)
        scale_part = jnp.sum(pre_grad * normed, axis=(0, 1, 2))
        shift_part = jnp.sum(pre_grad, axis=(0, 1, 2))
        sum_a, sum_b, scale_sum, shift_sum = lax.psum(
            (part_a, part_b, scale_part, shift_part), "slab"
        )
        branch = (
            rstd_c
            * (
                dnormed
                - jnp.repeat(sum_a / count_now, per_group)
                - normed * jnp.repeat(sum_b / count_now, per_group)
            )
            * mask_now[:, None, None, None]
        )
        result = (cotangent.astype(jnp.float32) + branch).astype(jnp.bfloat16)
        dx_list.append(result)
        embed_list.append(jnp.concatenate([scale_sum, shift_sum]) * embed_norm)
        cotangents.append(cotangent)
        if tick_index + 1 < tick_count:
            received = shifted(result, "pipe", -1)
    cot_all = jnp.stack(cotangents)
    shard_rows = weight_local.shape[0]
    hidden_all = jnp.stack([pad_cells(one_ext) for one_ext in hidden_exts])
    hidden_taps = tap_stack(hidden_all, frames, slab_rows, cells_wide, False)
    grad_term = jnp.einsum(
        "kfrwo,tkfrwi->oti", cot_all, hidden_taps, preferred_element_type=jnp.float32
    )
    grad_shard = lax.psum_scatter(
        (grad_term.reshape(lax.axis_size("dp") * shard_rows, -1) * weight_norm).astype(
            jnp.bfloat16
        ),
        "dp",
        scatter_dimension=0,
        tiled=True,
    ).astype(jnp.float32)
    weight_grad = lax.psum(grad_shard, "slab")
    input_grads = jnp.stack(dx_list)[None, :, None]
    embed_grad = jnp.stack(embed_list)[None, :, None]
    return (input_grads, weight_grad[None], embed_grad)


def solution(mesh):
    placed = (
        P("pipe", None, "dp", None, "slab", None, None),
        P(None, "dp", None, "slab", None, None),
        P("dp", None, "slab", None, None),
        P("pipe", "dp", None),
        P("pipe", None, None),
        P(None, "dp"),
        P(None, "dp"),
    )
    return jax.shard_map(
        local,
        mesh=mesh,
        in_specs=placed,
        out_specs=(
            P("pipe", None, "dp", None, "slab", None, None),
            P("pipe", "dp", None),
            P("pipe", None, "dp", None),
        ),
        check_vma=False,
    )
```

profile of v0, /device:TPU:8, one launch (start us, length us, event | category | flops | bytes accessed | tf_op | source)
XLA Modules:
  0.0 686.2 jit_solution(7426702432679894269)
XLA Ops:
  7.2 0.7 all-gather.3.cloned.1.call-update
  8.0 0.9 bitcast_select_fusion.2
  8.9 9.1 %collective-permute-start = (bf16[2,1,16,512]{3,2,1,0:T(8,128)(2,1)S(1)}, bf16[2,1,16,512]{3,2,1,0:T(8,128)(2,1)S(1)}, u32[]{:S(2)}, u32[]{:S(2)}) collective-permute-start(bf16[2,1,16,512]{3,2,1,0:T(8,128)(2,1)S(1)} %get-tuple-element.56), channel_id=1, source_target_pairs={{0,16},{16,32},{32,48},{48,64},{64,80},{80,96},{96,112},{1,17},{17... | collective-permute-start | bytes 98312 | tf_op jit(solution)/shard_map/ppermute | solution.py:18
  18.0 1.3 collective-permute-start.1
  19.3 0.7 convert_multiply_fusion.4
  20.1 1.0 fusion.43
  21.5 32.6 %all-reduce.6 = (f32[32]{0:T(128)S(1)}, f32[32]{0:T(128)S(1)}) all-reduce(f32[32]{0:T(128)S(1)} %reduce_sum.183, f32[32]{0:T(128)S(1)} %reduce_sum.181), channel_id=1, replica_groups=mesh['pipe'=2,'slab'=8,'dp'=16] {'slab'}, use_global_device_ids=true, to_apply=%region_5.0 | all-reduce | flops 64 | bytes 512 | tf_op jit(solution)/shard_map/psum | solution.py:118
  54.1 0.7 dynamic-slice_bitcast_fusion
  55.9 0.7 add_rsqrt_fusion.1
  57.3 0.7 constant_dynamic-update-slice_fusion.26
  58.0 0.6 constant_dynamic-update-slice_fusion.25
  58.6 0.6 constant_dynamic-update-slice_fusion.24
  59.3 0.6 constant_dynamic-update-slice_fusion.23
  59.9 0.6 constant_dynamic-update-slice_fusion.22
  60.6 0.6 constant_dynamic-update-slice_fusion.21
  61.2 0.6 constant_dynamic-update-slice_fusion.20
  61.9 0.6 constant_dynamic-update-slice_fusion.19
  62.5 0.6 constant_dynamic-update-slice_fusion.18
  63.1 0.6 constant_dynamic-update-slice_fusion.17
  63.8 0.6 constant_dynamic-update-slice_fusion.16
  64.4 0.6 constant_dynamic-update-slice_fusion.15
  65.1 0.6 constant_dynamic-update-slice_fusion.14
  65.7 0.6 constant_dynamic-update-slice_fusion.13
  66.4 0.6 constant_dynamic-update-slice_fusion.12
  67.0 0.6 constant_dynamic-update-slice_fusion.11
  67.7 0.6 constant_dynamic-update-slice_fusion.10
  68.3 0.6 constant_dynamic-update-slice_fusion.9
  68.9 0.6 constant_dynamic-update-slice_fusion.8
  69.6 0.6 constant_dynamic-update-slice_fusion.7
  70.2 0.6 constant_dynamic-update-slice_fusion.6
  70.9 0.6 constant_dynamic-update-slice_fusion.5
  71.5 0.6 constant_dynamic-update-slice_fusion.4
  72.2 0.6 constant_dynamic-update-slice_fusion.3
  72.8 0.6 constant_dynamic-update-slice_fusion.2
  73.4 0.6 constant_dynamic-update-slice_fusion.1
  74.1 0.6 constant_dynamic-update-slice_fusion
  74.7 94.1 %all-gather.3.cloned.1.call-done = bf16[1,512,13824]{2,1,0:T(8,128)(2,1)} async-done(((bf16[1,32,13824]{2,1,0:T(8,128)(2,1)}), bf16[1,512,13824]{2,1,0:T(8,128)(2,1)}) %all-gather.3.cloned.1.call-update) | async-done | bytes 14155792 | tf_op jit(solution)/shard_map/all_gather | solution.py:105
  168.8 18.7 %copy.101 = bf16[1,512,13824]{1,2,0:T(8,128)(2,1)} copy(bf16[1,512,13824]{2,1,0:T(8,128)(2,1)} %all-gather.3.cloned.1.call-done) | data formatting | bytes 28311552 | tf_op jit(solution)/shard_map/all_gather | solution.py:105
  187.5 10.0 %fusion.42 = (f32[512]{0:T(512)S(1)}, f32[512]{0:T(512)S(1)}, f32[512]{0:T(512)S(1)}, f32[512]{0:T(512)S(1)}, f32[2,2,16,512]{3,2,1,0:T(8,128)S(1)}) fusion(f32[512]{0:T(512)S(1)} %sub.59, f32[512]{0:T(512)S(1)} %mul.241, bf16[1,2,1,2,2,16,512]{6,5,4,3,2,1,0:T(8,128)(2,1)S(1)} %copy-done.3, f32[512]{0:T(512)S(1)} %bitcast.570, ...), kind=kOutput, calls=%fused_computation.194 | convolution fusion | flops 906655744 | bytes 16138248 | tf_op jit(solution)/shard_map/tfrwo,oti->frwi/dot_general | solution.py:139
  197.9 31.7 %all-reduce.5 = (f32[32]{0:T(128)S(1)}, f32[32]{0:T(128)S(1)}, f32[32]{0:T(128)S(1)}, f32[32]{0:T(128)S(1)}) all-reduce(f32[32]{0:T(128)S(1)} %reduce_sum.187, f32[32]{0:T(128)S(1)} %reduce_sum.185, f32[32]{0:T(128)S(1)} %reduce_sum.191, f32[32]{0:T(128)S(1)} %reduce_sum.189), channel_id=1, replica_groups=mesh['pipe'=2,'slab'=8,'dp'=16] {'slab'}, use_global_device_ids=true, to_apply=%region_11.12 | all-reduce | flops 128 | bytes 1024 | tf_op jit(solution)/shard_map/psum | solution.py:148
  229.6 0.6 broadcast_divide_fusion.3
  230.7 1.3 collective-permute-start.2
  232.0 1.8 collective-permute-done.2
  233.8 1.3 collective-permute-start.3
  235.1 1.3 collective-permute-start.4
  236.4 0.7 add_rsqrt_fusion
  237.4 8.5 %collective-permute-start.5 = (bf16[2,1,16,512]{3,2,1,0:T(8,128)(2,1)S(1)}, bf16[2,1,16,512]{3,2,1,0:T(8,128)(2,1)S(1)}, u32[]{:S(2)}, u32[]{:S(2)}) collective-permute-start(bf16[2,1,16,512]{3,2,1,0:T(8,128)(2,1)S(1)} %get-tuple-element.52), channel_id=1, source_target_pairs={{0,16},{16,32},{32,48},{48,64},{64,80},{80,96},{96,112},{1,17},{17... | collective-permute-start | bytes 98312 | tf_op jit(solution)/shard_map/ppermute | solution.py:18
  245.9 1.3 collective-permute-start.6
  247.9 9.4 %fusion.6 = f32[2,2,16,512]{3,2,0,1:T(8,128)S(1)} fusion(bf16[512,27,512,1,1]{0,2,3,4,1:T(8,128)(2,1)} %bitcast.562, bf16[27,2,2,16,512]{4,3,2,1,0:T(8,128)(2,1)S(1)} %constant_dynamic-update-slice_fusion.27), kind=kOutput, calls=%fused_computation.63 | convolution fusion | flops 905969664 | bytes 16056320 | tf_op jit(solution)/shard_map/tfrwo,oti->frwi/dot_general | solution.py:139
  257.5 8.7 %collective-permute-start.7 = (bf16[2,1,16,512]{3,2,1,0:T(8,128)(2,1)S(1)}, bf16[2,1,16,512]{3,2,1,0:T(8,128)(2,1)S(1)}, u32[]{:S(2)}, u32[]{:S(2)}) collective-permute-start(bf16[2,1,16,512]{3,2,1,0:T(8,128)(2,1)S(1)} %get-tuple-element.50), channel_id=1, source_target_pairs={{0,16},{16,32},{32,48},{48,64},{64,80},{80,96},{96,112},{1,17},{17... | collective-permute-start | bytes 98312 | tf_op jit(solution)/shard_map/ppermute | solution.py:18
  266.2 1.3 collective-permute-start.8
  267.8 9.0 %collective-permute-done.8 = bf16[2,1,16,512]{3,2,1,0:T(8,128)(2,1)S(1)} collective-permute-done((bf16[2,1,16,512]{3,2,1,0:T(8,128)(2,1)S(1)}, bf16[2,1,16,512]{3,2,1,0:T(8,128)(2,1)S(1)}, u32[]{:S(2)}, u32[]{:S(2)}) %collective-permute-start.8) | collective-permute-done | bytes 32800 | tf_op jit(solution)/shard_map/ppermute | solution.py:19
  278.0 1.7 copy-done.2
  279.7 9.1 %fusion = bf16[512,27,512]{0,2,1:T(8,128)(2,1)} fusion(bf16[27,2,2,2,16,512]{5,4,3,2,1,0:T(8,128)(2,1)} %copy-done.2, bf16[1,2,2,16,512]{4,3,2,1,0:T(8,128)(2,1)S(1)} %bitcast.564, bf16[1,2,2,16,512]{4,3,2,1,0:T(8,128)(2,1)S(1)} %get-tuple-element.46), kind=kOutput, calls=%fused_computation.1 | convolution fusion | flops 1826160640 | bytes 17825792 | tf_op jit(solution)/shard_map/kfrwo,tkfrwi->oti/dot_general | solution.py:170
  288.8 18.6 %copy.108 = bf16[512,13824]{1,0:T(8,128)(2,1)} copy(bf16[512,13824]{0,1:T(8,128)(2,1)} %bitcast.563) | data formatting | bytes 28311552 | tf_op jit(solution)/shard_map/convert_element_type | solution.py:174
  307.5 193.0 %reduce-scatter.2.cloned.1.call-done = bf16[32,13824]{1,0:T(8,128)(2,1)} async-done(((bf16[512,13824]{1,0:T(8,128)(2,1)}), bf16[32,13824]{1,0:T(8,128)(2,1)}) %reduce-scatter.2.cloned.1.call-update) | async-done | bytes 884752 | tf_op jit(solution)/shard_map/reduce_scatter | solution.py:173
  500.5 2.5 bitcast_convert_fusion
  503.5 35.7 %all-reduce.4 = (f32[32]{0:T(128)S(1)}, f32[32]{0:T(128)S(1)}, f32[1,512]{1,0:T(1,128)S(1)}, f32[1,512]{1,0:T(1,128)S(1)}, f32[1,512]{1,0:T(1,128)S(1)}, /*index=5*/f32[1,512]{1,0:T(1,128)S(1)}) all-reduce(f32[32]{0:T(128)S(1)} %reduce_sum.195, f32[32]{0:T(128)S(1)} %reduce_sum.193, ...), channel_id=1, replica_groups=mesh['pipe'=2,'slab'=8,'dp'=16] {'slab'}, use_global_device_ids=true, to_apply=%region_23.24 | all-reduce | flops 2112 | bytes 16896 | tf_op jit(solution)/shard_map/psum | solution.py:148
  539.2 0.6 broadcast_in_dim.47
  539.8 0.6 broadcast_divide_fusion.1
  540.6 0.7 broadcast_divide_fusion
  541.5 0.7 maximum_bitcast_fusion
  542.2 134.7 %all-reduce.9.cloned.1.call-done = f32[1,32,13824]{2,1,0:T(8,128)} async-done(((f32[1,32,13824]{2,1,0:T(8,128)}), f32[1,32,13824]{2,1,0:T(8,128)}) %all-reduce.9.cloned.1.call-update) | async-done | bytes 1769488 | tf_op jit(solution)/shard_map/psum | solution.py:181
  676.9 2.8 copy.209
  (131 shorter events, 6.2 us)
Async XLA Ops:
  7.2 48.2 %copy-start = (bf16[1,1000,1024]{2,1,0:T(8,128)(2,1)S(1)}, bf16[1,1000,1024]{2,1,0:T(8,128)(2,1)}, u32[]{:S(2)}) copy-start(bf16[1,1000,1024]{2,1,0:T(8,128)(2,1)} %param.11) | copy-start | bytes 6144004
  7.2 161.6 %all-gather.3.cloned.1.call-start = ((), (), s32[]{:S(2)}) async-start(), calls=%async_computation.3 | async-start | bytes 15040512 | tf_op jit(solution)/shard_map/all_gather | solution.py:105
  7.9 492.6 %reduce-scatter.2.cloned.1.call-start = ((), (), s32[]{:S(2)}) async-start(), calls=%async_computation.1 | async-start | bytes 15040512 | tf_op jit(solution)/shard_map/reduce_scatter | solution.py:173
  8.9 48.4 %collective-permute-start = (bf16[2,1,16,512]{3,2,1,0:T(8,128)(2,1)S(1)}, bf16[2,1,16,512]{3,2,1,0:T(8,128)(2,1)S(1)}, u32[]{:S(2)}, u32[]{:S(2)}) collective-permute-start(bf16[2,1,16,512]{3,2,1,0:T(8,128)(2,1)S(1)} %get-tuple-element.56), channel_id=1, source_target_pairs={{0,16},{16,32},{32,48},{48,64},{64,80},{80,96},{96,112},{1,17},{17... | collective-permute-start | bytes 98312 | tf_op jit(solution)/shard_map/ppermute | solution.py:18
  18.0 39.3 %collective-permute-start.1 = (bf16[2,1,16,512]{3,2,1,0:T(8,128)(2,1)S(1)}, bf16[2,1,16,512]{3,2,1,0:T(8,128)(2,1)S(1)}, u32[]{:S(2)}, u32[]{:S(2)}) collective-permute-start(bf16[2,1,16,512]{3,2,1,0:T(8,128)(2,1)S(1)} %get-tuple-element.57), channel_id=1, source_target_pairs={{16,0},{32,16},{48,32},{64,48},{80,64},{96,80},{112,96},{17,1},{33... | collective-permute-start | bytes 98312 | tf_op jit(solution)/shard_map/ppermute | solution.py:19
  55.4 10.3 %copy-start.4 = (bf16[2,1,2,2,16,512]{5,4,3,2,1,0:T(8,128)(2,1)S(1)}, bf16[2,1,2,2,16,512]{5,4,3,2,1,0:T(8,128)(2,1)}, u32[]{:S(2)}) copy-start(bf16[2,1,2,2,16,512]{5,4,3,2,1,0:T(8,128)(2,1)} %param.8) | copy-start | bytes 393220
  55.4 10.3 %copy-start.5 = (bf16[1,2,2,16,512]{4,3,2,1,0:T(8,128)(2,1)S(1)}, bf16[1,2,2,16,512]{4,3,2,1,0:T(8,128)(2,1)}, u32[]{:S(2)}) copy-start(bf16[1,2,2,16,512]{4,3,2,1,0:T(8,128)(2,1)} %param.9) | copy-start | bytes 196612
  74.7 112.8 %copy-start.3 = (bf16[1,2,1,2,2,16,512]{6,5,4,3,2,1,0:T(8,128)(2,1)S(1)}, bf16[1,2,1,2,2,16,512]{6,5,4,3,2,1,0:T(8,128)(2,1)}, u32[]{:S(2)}) copy-start(bf16[1,2,1,2,2,16,512]{6,5,4,3,2,1,0:T(8,128)(2,1)} %param.7) | copy-start | bytes 393220
  230.7 3.1 collective-permute-start.2
  233.8 13.3 %collective-permute-start.3 = (bf16[2,1,16,512]{3,2,1,0:T(8,128)(2,1)S(1)}, bf16[2,1,16,512]{3,2,1,0:T(8,128)(2,1)S(1)}, u32[]{:S(2)}, u32[]{:S(2)}) collective-permute-start(bf16[2,1,16,512]{3,2,1,0:T(8,128)(2,1)S(1)} %get-tuple-element.54), channel_id=1, source_target_pairs={{0,16},{16,32},{32,48},{48,64},{64,80},{80,96},{96,112},{1,17},{17... | collective-permute-start | bytes 98312 | tf_op jit(solution)/shard_map/ppermute | solution.py:18
  235.1 12.0 %collective-permute-start.4 = (bf16[2,1,16,512]{3,2,1,0:T(8,128)(2,1)S(1)}, bf16[2,1,16,512]{3,2,1,0:T(8,128)(2,1)S(1)}, u32[]{:S(2)}, u32[]{:S(2)}) collective-permute-start(bf16[2,1,16,512]{3,2,1,0:T(8,128)(2,1)S(1)} %get-tuple-element.55), channel_id=1, source_target_pairs={{16,0},{32,16},{48,32},{64,48},{80,64},{96,80},{112,96},{17,1},{33... | collective-permute-start | bytes 98312 | tf_op jit(solution)/shard_map/ppermute | solution.py:19
  237.4 30.1 %collective-permute-start.5 = (bf16[2,1,16,512]{3,2,1,0:T(8,128)(2,1)S(1)}, bf16[2,1,16,512]{3,2,1,0:T(8,128)(2,1)S(1)}, u32[]{:S(2)}, u32[]{:S(2)}) collective-permute-start(bf16[2,1,16,512]{3,2,1,0:T(8,128)(2,1)S(1)} %get-tuple-element.52), channel_id=1, source_target_pairs={{0,16},{16,32},{32,48},{48,64},{64,80},{80,96},{96,112},{1,17},{17... | collective-permute-start | bytes 98312 | tf_op jit(solution)/shard_map/ppermute | solution.py:18
  245.9 21.6 %collective-permute-start.6 = (bf16[2,1,16,512]{3,2,1,0:T(8,128)(2,1)S(1)}, bf16[2,1,16,512]{3,2,1,0:T(8,128)(2,1)S(1)}, u32[]{:S(2)}, u32[]{:S(2)}) collective-permute-start(bf16[2,1,16,512]{3,2,1,0:T(8,128)(2,1)S(1)} %get-tuple-element.53), channel_id=1, source_target_pairs={{16,0},{32,16},{48,32},{64,48},{80,64},{96,80},{112,96},{17,1},{33... | collective-permute-start | bytes 98312 | tf_op jit(solution)/shard_map/ppermute | solution.py:19
  257.5 10.3 %collective-permute-start.7 = (bf16[2,1,16,512]{3,2,1,0:T(8,128)(2,1)S(1)}, bf16[2,1,16,512]{3,2,1,0:T(8,128)(2,1)S(1)}, u32[]{:S(2)}, u32[]{:S(2)}) collective-permute-start(bf16[2,1,16,512]{3,2,1,0:T(8,128)(2,1)S(1)} %get-tuple-element.50), channel_id=1, source_target_pairs={{0,16},{16,32},{32,48},{48,64},{64,80},{80,96},{96,112},{1,17},{17... | collective-permute-start | bytes 98312 | tf_op jit(solution)/shard_map/ppermute | solution.py:18
  266.2 10.6 %collective-permute-start.8 = (bf16[2,1,16,512]{3,2,1,0:T(8,128)(2,1)S(1)}, bf16[2,1,16,512]{3,2,1,0:T(8,128)(2,1)S(1)}, u32[]{:S(2)}, u32[]{:S(2)}) collective-permute-start(bf16[2,1,16,512]{3,2,1,0:T(8,128)(2,1)S(1)} %get-tuple-element.51), channel_id=1, source_target_pairs={{16,0},{32,16},{48,32},{64,48},{80,64},{96,80},{112,96},{17,1},{33... | collective-permute-start | bytes 98312 | tf_op jit(solution)/shard_map/ppermute | solution.py:19
  278.0 1.7 copy-start.2
  307.5 369.4 %all-reduce.9.cloned.1.call-start = ((), (), s32[]{:S(2)}) async-start(), calls=%async_computation.2 | async-start | bytes 3538944 | tf_op jit(solution)/shard_map/psum | solution.py:181
  541.5 138.2 %copy-start.1 = (bf16[1,1000,1024]{2,1,0:T(8,128)(2,1)S(1)}, bf16[1,1000,1024]{2,1,0:T(8,128)(2,1)}, u32[]{:S(2)}) copy-start(bf16[1,1000,1024]{2,1,0:T(8,128)(2,1)} %param.11) | copy-start | bytes 6144004
Sparse Core Ops, SparseCore 0:
  9.8 158.9 all-gather.2
  307.6 192.8 reduce-scatter.1
  503.8 173.0 all-reduce.8
where the time goes:
time: 688 us; the launch traced here: 686 us
  waiting for transfers between devices  434 us (63%)
  blocking collectives  100 us (15%)
  local copies, waits for them, and re-layouts  61.5 us (9%)
  starting transfers between devices  34.2 us (5%)
  matrix products  28.9 us (4%)
  between operations  14.6 us (2%)
  other arithmetic  13.5 us (2%)
    reduce_scatter x1, waiting for transfers between devices, local(): lax.psum_scatter((grad_term.reshape(lax.axis_size('dp') * shard_rows, -1)...  193 us
    psum x1, waiting for transfers between devices, local(): weight_grad = lax.psum(grad_shard, 'slab')  135 us
    all_gather x1, waiting for transfers between devices, local(): lax.all_gather(weight_local, 'dp', axis=0, tiled=True)  94.1 us
    psum x2, blocking collectives, local(): lax.psum((part_a, part_b, scale_part, shift_part), 'slab')  67.4 us
    psum x1, blocking collectives, local(): moment_one, moment_two = lax.psum((part_one, part_two), 'slab')  32.6 us
    ppermute x4, starting transfers between devices, extended(): before = lax.ppermute(last, axis, up)  27.6 us
    unnamed x60, local copies, waits for them, and re-layouts  19.8 us
    dot_general x2, matrix products, local(): jnp.einsum('tfrwo,oti->frwi', tap_slices, full_weight, preferred_element_...  19.4 us
  transfers between devices with their start and end apart: 12, of which 6 were waited for; matrix products, arithmetic and copies ran while one was open for 6% of the time, Pallas kernels for 0%

commit v1 on v0

--- a/solution.py
+++ b/solution.py
@@ -178,7 +178,8 @@
         scatter_dimension=0,
         tiled=True,
     ).astype(jnp.float32)
-    weight_grad = lax.psum(grad_shard, "slab")
+    upper = lax.all_gather(grad_shard, "slab")
+    weight_grad = jnp.sum(upper, axis=0)
     input_grads = jnp.stack(dx_list)[None, :, None]
     embed_grad = jnp.stack(embed_list)[None, :, None]
     return (input_grads, weight_grad[None], embed_grad)

time: 688 us -> 787 us (1.14)
  waiting for transfers between devices: 434 us -> 528 us
    all_gather x0 -> x1, waiting for transfers between devices: none -> 229 us  [local(): upper = lax.all_gather(grad_shard, 'slab')]
    psum x1 -> x0, waiting for transfers between devices: 135 us -> none  [local(): weight_grad = lax.psum(grad_shard, 'slab')]
    unnamed x60 -> x59, local copies, waits for them, and re-layouts: 19.8 us -> 17 us
  transfers between devices with their start and end apart: 12 -> 12, of which waited for: 6 -> 6; matrix products, arithmetic and copies ran while one was open for 6% -> 5% of each run, Pallas kernels for 0% -> 0%
where the time goes in v1:
time: 787 us; the launch traced here: 785 us
  waiting for transfers between devices  528 us (67%)
  blocking collectives  99.5 us (13%)
  local copies, waits for them, and re-layouts  58.7 us (7%)
  starting transfers between devices  34.2 us (4%)
  matrix products  28.9 us (4%)
  other arithmetic  20.8 us (3%)
  between operations  14.5 us (2%)
    all_gather x1, waiting for transfers between devices, local(): upper = lax.all_gather(grad_shard, 'slab')  229 us
    reduce_scatter x1, waiting for transfers between devices, local(): lax.psum_scatter((grad_term.reshape(lax.axis_size('dp') * shard_rows, -1)...  193 us
    all_gather x1, waiting for transfers between devices, local(): lax.all_gather(weight_local, 'dp', axis=0, tiled=True)  94.1 us
    psum x2, blocking collectives, local(): lax.psum((part_a, part_b, scale_part, shift_part), 'slab')  66.9 us
    psum x1, blocking collectives, local(): moment_one, moment_two = lax.psum((part_one, part_two), 'slab')  32.6 us
    ppermute x4, starting transfers between devices, extended(): before = lax.ppermute(last, axis, up)  27.6 us
    dot_general x2, matrix products, local(): jnp.einsum('tfrwo,oti->frwi', tap_slices, full_weight, preferred_element_...  19.4 us
    all_gather x1, local copies, waits for them, and re-layouts, local(): lax.all_gather(weight_local, 'dp', axis=0, tiled=True)  18.7 us
  transfers between devices with their start and end apart: 12, of which 6 were waited for; matrix products, arithmetic and copies ran while one was open for 5% of the time, Pallas kernels for 0%

profile of v1, /device:TPU:8, one launch (start us, length us, event | category | flops | bytes accessed | tf_op | source)
XLA Modules:
  0.0 785.0 jit_solution(15311315669809999408)
XLA Ops:
  7.2 0.7 all-gather.5.cloned.1.call-update
  8.0 0.9 bitcast_select_fusion.2
  8.9 9.1 %collective-permute-start = (bf16[2,1,16,512]{3,2,1,0:T(8,128)(2,1)S(1)}, bf16[2,1,16,512]{3,2,1,0:T(8,128)(2,1)S(1)}, u32[]{:S(2)}, u32[]{:S(2)}) collective-permute-start(bf16[2,1,16,512]{3,2,1,0:T(8,128)(2,1)S(1)} %get-tuple-element.56), channel_id=1, source_target_pairs={{0,16},{16,32},{32,48},{48,64},{64,80},{80,96},{96,112},{1,17},{17... | collective-permute-start | bytes 98312 | tf_op jit(solution)/shard_map/ppermute | solution.py:18
  18.0 1.3 collective-permute-start.1
  19.3 0.7 convert_multiply_fusion.4
  20.1 1.0 fusion.43
  21.5 32.6 %all-reduce.6 = (f32[32]{0:T(128)S(1)}, f32[32]{0:T(128)S(1)}) all-reduce(f32[32]{0:T(128)S(1)} %reduce_sum.192, f32[32]{0:T(128)S(1)} %reduce_sum.190), channel_id=1, replica_groups=mesh['pipe'=2,'slab'=8,'dp'=16] {'slab'}, use_global_device_ids=true, to_apply=%region_5.0 | all-reduce | flops 64 | bytes 512 | tf_op jit(solution)/shard_map/psum | solution.py:118
  54.1 0.7 dynamic-slice_bitcast_fusion
  55.9 0.7 add_rsqrt_fusion.1
  57.3 0.7 constant_dynamic-update-slice_fusion.26
  58.0 0.6 constant_dynamic-update-slice_fusion.25
  58.6 0.6 constant_dynamic-update-slice_fusion.24
  59.3 0.6 constant_dynamic-update-slice_fusion.23
  59.9 0.6 constant_dynamic-update-slice_fusion.22
  60.6 0.6 constant_dynamic-update-slice_fusion.21
  61.2 0.6 constant_dynamic-update-slice_fusion.20
  61.9 0.6 constant_dynamic-update-slice_fusion.19
  62.5 0.6 constant_dynamic-update-slice_fusion.18
  63.1 0.6 constant_dynamic-update-slice_fusion.17
  63.8 0.6 constant_dynamic-update-slice_fusion.16
  64.4 0.6 constant_dynamic-update-slice_fusion.15
  65.1 0.6 constant_dynamic-update-slice_fusion.14
  65.7 0.6 constant_dynamic-update-slice_fusion.13
  66.4 0.6 constant_dynamic-update-slice_fusion.12
  67.0 0.6 constant_dynamic-update-slice_fusion.11
  67.7 0.6 constant_dynamic-update-slice_fusion.10
  68.3 0.6 constant_dynamic-update-slice_fusion.9
  68.9 0.6 constant_dynamic-update-slice_fusion.8
  69.6 0.6 constant_dynamic-update-slice_fusion.7
  70.2 0.6 constant_dynamic-update-slice_fusion.6
  70.9 0.6 constant_dynamic-update-slice_fusion.5
  71.5 0.6 constant_dynamic-update-slice_fusion.4
  72.2 0.6 constant_dynamic-update-slice_fusion.3
  72.8 0.6 constant_dynamic-update-slice_fusion.2
  73.4 0.6 constant_dynamic-update-slice_fusion.1
  74.1 0.6 constant_dynamic-update-slice_fusion
  74.7 94.1 %all-gather.5.cloned.1.call-done = bf16[1,512,13824]{2,1,0:T(8,128)(2,1)} async-done(((bf16[1,32,13824]{2,1,0:T(8,128)(2,1)}), bf16[1,512,13824]{2,1,0:T(8,128)(2,1)}) %all-gather.5.cloned.1.call-update) | async-done | bytes 14155792 | tf_op jit(solution)/shard_map/all_gather | solution.py:105
  168.8 18.7 %copy.100 = bf16[1,512,13824]{1,2,0:T(8,128)(2,1)} copy(bf16[1,512,13824]{2,1,0:T(8,128)(2,1)} %all-gather.5.cloned.1.call-done) | data formatting | bytes 28311552 | tf_op jit(solution)/shard_map/all_gather | solution.py:105
  187.5 10.0 %fusion.42 = (f32[512]{0:T(512)S(1)}, f32[512]{0:T(512)S(1)}, f32[512]{0:T(512)S(1)}, f32[512]{0:T(512)S(1)}, f32[2,2,16,512]{3,2,1,0:T(8,128)S(1)}) fusion(f32[512]{0:T(512)S(1)} %sub.59, f32[512]{0:T(512)S(1)} %mul.241, bf16[1,2,1,2,2,16,512]{6,5,4,3,2,1,0:T(8,128)(2,1)S(1)} %copy-done.3, f32[512]{0:T(512)S(1)} %bitcast.571, ...), kind=kOutput, calls=%fused_computation.193 | convolution fusion | flops 906655744 | bytes 16138248 | tf_op jit(solution)/shard_map/tfrwo,oti->frwi/dot_general | solution.py:139
  197.9 31.7 %all-reduce.5 = (f32[32]{0:T(128)S(1)}, f32[32]{0:T(128)S(1)}, f32[32]{0:T(128)S(1)}, f32[32]{0:T(128)S(1)}) all-reduce(f32[32]{0:T(128)S(1)} %reduce_sum.196, f32[32]{0:T(128)S(1)} %reduce_sum.194, f32[32]{0:T(128)S(1)} %reduce_sum.200, f32[32]{0:T(128)S(1)} %reduce_sum.198), channel_id=1, replica_groups=mesh['pipe'=2,'slab'=8,'dp'=16] {'slab'}, use_global_device_ids=true, to_apply=%region_11.12 | all-reduce | flops 128 | bytes 1024 | tf_op jit(solution)/shard_map/psum | solution.py:148
  229.6 0.6 broadcast_divide_fusion.3
  230.7 1.3 collective-permute-start.2
  232.0 1.8 collective-permute-done.2
  233.8 1.3 collective-permute-start.3
  235.1 1.3 collective-permute-start.4
  236.4 0.7 add_rsqrt_fusion
  237.4 8.5 %collective-permute-start.5 = (bf16[2,1,16,512]{3,2,1,0:T(8,128)(2,1)S(1)}, bf16[2,1,16,512]{3,2,1,0:T(8,128)(2,1)S(1)}, u32[]{:S(2)}, u32[]{:S(2)}) collective-permute-start(bf16[2,1,16,512]{3,2,1,0:T(8,128)(2,1)S(1)} %get-tuple-element.52), channel_id=1, source_target_pairs={{0,16},{16,32},{32,48},{48,64},{64,80},{80,96},{96,112},{1,17},{17... | collective-permute-start | bytes 98312 | tf_op jit(solution)/shard_map/ppermute | solution.py:18
  245.9 1.3 collective-permute-start.6
  247.9 9.4 %fusion.6 = f32[2,2,16,512]{3,2,0,1:T(8,128)S(1)} fusion(bf16[512,27,512,1,1]{0,2,3,4,1:T(8,128)(2,1)} %bitcast.561, bf16[27,2,2,16,512]{4,3,2,1,0:T(8,128)(2,1)S(1)} %constant_dynamic-update-slice_fusion.27), kind=kOutput, calls=%fused_computation.63 | convolution fusion | flops 905969664 | bytes 16056320 | tf_op jit(solution)/shard_map/tfrwo,oti->frwi/dot_general | solution.py:139
  257.5 8.7 %collective-permute-start.7 = (bf16[2,1,16,512]{3,2,1,0:T(8,128)(2,1)S(1)}, bf16[2,1,16,512]{3,2,1,0:T(8,128)(2,1)S(1)}, u32[]{:S(2)}, u32[]{:S(2)}) collective-permute-start(bf16[2,1,16,512]{3,2,1,0:T(8,128)(2,1)S(1)} %get-tuple-element.50), channel_id=1, source_target_pairs={{0,16},{16,32},{32,48},{48,64},{64,80},{80,96},{96,112},{1,17},{17... | collective-permute-start | bytes 98312 | tf_op jit(solution)/shard_map/ppermute | solution.py:18
  266.2 1.3 collective-permute-start.8
  267.8 9.0 %collective-permute-done.8 = bf16[2,1,16,512]{3,2,1,0:T(8,128)(2,1)S(1)} collective-permute-done((bf16[2,1,16,512]{3,2,1,0:T(8,128)(2,1)S(1)}, bf16[2,1,16,512]{3,2,1,0:T(8,128)(2,1)S(1)}, u32[]{:S(2)}, u32[]{:S(2)}) %collective-permute-start.8) | collective-permute-done | bytes 32800 | tf_op jit(solution)/shard_map/ppermute | solution.py:19
  278.0 1.7 copy-done.2
  279.7 9.1 %fusion = bf16[512,27,512]{0,2,1:T(8,128)(2,1)} fusion(bf16[27,2,2,2,16,512]{5,4,3,2,1,0:T(8,128)(2,1)} %copy-done.2, bf16[1,2,2,16,512]{4,3,2,1,0:T(8,128)(2,1)S(1)} %bitcast.564, bf16[1,2,2,16,512]{4,3,2,1,0:T(8,128)(2,1)S(1)} %get-tuple-element.46), kind=kOutput, calls=%fused_computation.1 | convolution fusion | flops 1826160640 | bytes 17825792 | tf_op jit(solution)/shard_map/kfrwo,tkfrwi->oti/dot_general | solution.py:170
  288.8 18.6 %copy.107 = bf16[512,13824]{1,0:T(8,128)(2,1)} copy(bf16[512,13824]{0,1:T(8,128)(2,1)} %bitcast.562) | data formatting | bytes 28311552 | tf_op jit(solution)/shard_map/convert_element_type | solution.py:174
  307.5 193.0 %reduce-scatter.2.cloned.1.call-done = bf16[32,13824]{1,0:T(8,128)(2,1)} async-done(((bf16[512,13824]{1,0:T(8,128)(2,1)}), bf16[32,13824]{1,0:T(8,128)(2,1)}) %reduce-scatter.2.cloned.1.call-update) | async-done | bytes 884752 | tf_op jit(solution)/shard_map/reduce_scatter | solution.py:173
  500.5 2.5 all_gather.16
  503.5 35.2 %all-reduce.4 = (f32[32]{0:T(128)S(1)}, f32[32]{0:T(128)S(1)}, f32[1,512]{1,0:T(1,128)S(1)}, f32[1,512]{1,0:T(1,128)S(1)}, f32[1,512]{1,0:T(1,128)S(1)}, /*index=5*/f32[1,512]{1,0:T(1,128)S(1)}) all-reduce(f32[32]{0:T(128)S(1)} %reduce_sum.204, f32[32]{0:T(128)S(1)} %reduce_sum.202, ...), channel_id=1, replica_groups=mesh['pipe'=2,'slab'=8,'dp'=16] {'slab'}, use_global_device_ids=true, to_apply=%region_23.24 | all-reduce | flops 2112 | bytes 16896 | tf_op jit(solution)/shard_map/psum | solution.py:148
  538.7 0.6 broadcast_in_dim.47
  539.3 0.6 broadcast_divide_fusion.1
  540.1 0.7 broadcast_divide_fusion
  541.0 0.7 maximum_bitcast_fusion
  541.7 229.5 %all-gather.7.cloned.1.call-done = f32[256,13824]{1,0:T(8,128)} async-done(((f32[32,13824]{1,0:T(8,128)}), f32[256,13824]{1,0:T(8,128)}) %all-gather.7.cloned.1.call-update) | async-done | bytes 14155792 | tf_op jit(solution)/shard_map/all_gather | solution.py:181
  771.2 7.3 reduce_sum.205
  (131 shorter events, 6.2 us)
Async XLA Ops:
  7.2 48.2 %copy-start = (bf16[1,1000,1024]{2,1,0:T(8,128)(2,1)S(1)}, bf16[1,1000,1024]{2,1,0:T(8,128)(2,1)}, u32[]{:S(2)}) copy-start(bf16[1,1000,1024]{2,1,0:T(8,128)(2,1)} %param.11) | copy-start | bytes 6144004
  7.2 161.6 %all-gather.5.cloned.1.call-start = ((), (), s32[]{:S(2)}) async-start(), calls=%async_computation.2 | async-start | bytes 15040512 | tf_op jit(solution)/shard_map/all_gather | solution.py:105
  7.9 492.6 %reduce-scatter.2.cloned.1.call-start = ((), (), s32[]{:S(2)}) async-start(), calls=%async_computation.1 | async-start | bytes 15040512 | tf_op jit(solution)/shard_map/reduce_scatter | solution.py:173
  8.9 48.4 %collective-permute-start = (bf16[2,1,16,512]{3,2,1,0:T(8,128)(2,1)S(1)}, bf16[2,1,16,512]{3,2,1,0:T(8,128)(2,1)S(1)}, u32[]{:S(2)}, u32[]{:S(2)}) collective-permute-start(bf16[2,1,16,512]{3,2,1,0:T(8,128)(2,1)S(1)} %get-tuple-element.56), channel_id=1, source_target_pairs={{0,16},{16,32},{32,48},{48,64},{64,80},{80,96},{96,112},{1,17},{17... | collective-permute-start | bytes 98312 | tf_op jit(solution)/shard_map/ppermute | solution.py:18
  18.0 39.3 %collective-permute-start.1 = (bf16[2,1,16,512]{3,2,1,0:T(8,128)(2,1)S(1)}, bf16[2,1,16,512]{3,2,1,0:T(8,128)(2,1)S(1)}, u32[]{:S(2)}, u32[]{:S(2)}) collective-permute-start(bf16[2,1,16,512]{3,2,1,0:T(8,128)(2,1)S(1)} %get-tuple-element.57), channel_id=1, source_target_pairs={{16,0},{32,16},{48,32},{64,48},{80,64},{96,80},{112,96},{17,1},{33... | collective-permute-start | bytes 98312 | tf_op jit(solution)/shard_map/ppermute | solution.py:19
  55.4 10.3 %copy-start.4 = (bf16[2,1,2,2,16,512]{5,4,3,2,1,0:T(8,128)(2,1)S(1)}, bf16[2,1,2,2,16,512]{5,4,3,2,1,0:T(8,128)(2,1)}, u32[]{:S(2)}) copy-start(bf16[2,1,2,2,16,512]{5,4,3,2,1,0:T(8,128)(2,1)} %param.8) | copy-start | bytes 393220
  55.4 10.3 %copy-start.5 = (bf16[1,2,2,16,512]{4,3,2,1,0:T(8,128)(2,1)S(1)}, bf16[1,2,2,16,512]{4,3,2,1,0:T(8,128)(2,1)}, u32[]{:S(2)}) copy-start(bf16[1,2,2,16,512]{4,3,2,1,0:T(8,128)(2,1)} %param.9) | copy-start | bytes 196612
  74.7 112.8 %copy-start.3 = (bf16[1,2,1,2,2,16,512]{6,5,4,3,2,1,0:T(8,128)(2,1)S(1)}, bf16[1,2,1,2,2,16,512]{6,5,4,3,2,1,0:T(8,128)(2,1)}, u32[]{:S(2)}) copy-start(bf16[1,2,1,2,2,16,512]{6,5,4,3,2,1,0:T(8,128)(2,1)} %param.7) | copy-start | bytes 393220
  230.7 3.1 collective-permute-start.2
  233.8 13.3 %collective-permute-start.3 = (bf16[2,1,16,512]{3,2,1,0:T(8,128)(2,1)S(1)}, bf16[2,1,16,512]{3,2,1,0:T(8,128)(2,1)S(1)}, u32[]{:S(2)}, u32[]{:S(2)}) collective-permute-start(bf16[2,1,16,512]{3,2,1,0:T(8,128)(2,1)S(1)} %get-tuple-element.54), channel_id=1, source_target_pairs={{0,16},{16,32},{32,48},{48,64},{64,80},{80,96},{96,112},{1,17},{17... | collective-permute-start | bytes 98312 | tf_op jit(solution)/shard_map/ppermute | solution.py:18
  235.1 12.0 %collective-permute-start.4 = (bf16[2,1,16,512]{3,2,1,0:T(8,128)(2,1)S(1)}, bf16[2,1,16,512]{3,2,1,0:T(8,128)(2,1)S(1)}, u32[]{:S(2)}, u32[]{:S(2)}) collective-permute-start(bf16[2,1,16,512]{3,2,1,0:T(8,128)(2,1)S(1)} %get-tuple-element.55), channel_id=1, source_target_pairs={{16,0},{32,16},{48,32},{64,48},{80,64},{96,80},{112,96},{17,1},{33... | collective-permute-start | bytes 98312 | tf_op jit(solution)/shard_map/ppermute | solution.py:19
  237.4 30.1 %collective-permute-start.5 = (bf16[2,1,16,512]{3,2,1,0:T(8,128)(2,1)S(1)}, bf16[2,1,16,512]{3,2,1,0:T(8,128)(2,1)S(1)}, u32[]{:S(2)}, u32[]{:S(2)}) collective-permute-start(bf16[2,1,16,512]{3,2,1,0:T(8,128)(2,1)S(1)} %get-tuple-element.52), channel_id=1, source_target_pairs={{0,16},{16,32},{32,48},{48,64},{64,80},{80,96},{96,112},{1,17},{17... | collective-permute-start | bytes 98312 | tf_op jit(solution)/shard_map/ppermute | solution.py:18
  245.9 21.6 %collective-permute-start.6 = (bf16[2,1,16,512]{3,2,1,0:T(8,128)(2,1)S(1)}, bf16[2,1,16,512]{3,2,1,0:T(8,128)(2,1)S(1)}, u32[]{:S(2)}, u32[]{:S(2)}) collective-permute-start(bf16[2,1,16,512]{3,2,1,0:T(8,128)(2,1)S(1)} %get-tuple-element.53), channel_id=1, source_target_pairs={{16,0},{32,16},{48,32},{64,48},{80,64},{96,80},{112,96},{17,1},{33... | collective-permute-start | bytes 98312 | tf_op jit(solution)/shard_map/ppermute | solution.py:19
  257.5 10.3 %collective-permute-start.7 = (bf16[2,1,16,512]{3,2,1,0:T(8,128)(2,1)S(1)}, bf16[2,1,16,512]{3,2,1,0:T(8,128)(2,1)S(1)}, u32[]{:S(2)}, u32[]{:S(2)}) collective-permute-start(bf16[2,1,16,512]{3,2,1,0:T(8,128)(2,1)S(1)} %get-tuple-element.50), channel_id=1, source_target_pairs={{0,16},{16,32},{32,48},{48,64},{64,80},{80,96},{96,112},{1,17},{17... | collective-permute-start | bytes 98312 | tf_op jit(solution)/shard_map/ppermute | solution.py:18
  266.2 10.6 %collective-permute-start.8 = (bf16[2,1,16,512]{3,2,1,0:T(8,128)(2,1)S(1)}, bf16[2,1,16,512]{3,2,1,0:T(8,128)(2,1)S(1)}, u32[]{:S(2)}, u32[]{:S(2)}) collective-permute-start(bf16[2,1,16,512]{3,2,1,0:T(8,128)(2,1)S(1)} %get-tuple-element.51), channel_id=1, source_target_pairs={{16,0},{32,16},{48,32},{64,48},{80,64},{96,80},{112,96},{17,1},{33... | collective-permute-start | bytes 98312 | tf_op jit(solution)/shard_map/ppermute | solution.py:19
  278.0 1.7 copy-start.2
  307.5 463.7 %all-gather.7.cloned.1.call-start = ((), (), s32[]{:S(2)}) async-start(), calls=%async_computation.3 | async-start | bytes 15925248 | tf_op jit(solution)/shard_map/all_gather | solution.py:181
  771.2 7.3 copy-start.1
Sparse Core Ops, SparseCore 0:
  9.8 158.9 all-gather.4
  307.6 192.8 reduce-scatter.1
  503.7 267.3 all-gather.6
